TPU v7x, 256 devices: a whole 4x4x8 slice. The times are simulated.
256 devices in a mesh: tiles: 64 (over y, z, core), rep: 4 (over x).
Axes of the slice: x: 4, y: 4, z: 8, core: 2. Of those that a mesh axis runs over, the one named last changes fastest.
Arguments:
- trailing_tiles: float32 [5120, 256, 256], P(('tiles', 'rep')), may hold values from -6 to 6
- panel_rows: float32 [128, 256, 512], P('tiles'), may hold values from -3 to 3
- pivot_blocks: float32 [2, 256, 256], replicated
- coupling: float32 [256, 256], replicated, may hold values from -0.1875 to 0.1875
- row_ids: int32 [128], replicated, may hold values from 2 to 96, as said below
- membership: int32 [64, 24], replicated, may hold values from 2 to 96, as said below
- tile_pairs: int32 [5120, 2], P(('tiles', 'rep')), may hold values from 0 to 24, as said below
Outputs:
- updated_tiles: float32 [5120, 256, 256], P(('tiles', 'rep'))
- factors: float32 [128, 256, 512], P('tiles')
- pivot_diag: float32 [2, 256], replicated
Inputs may be any that keep to these rules, and one draw needn't show every extreme that they name: `row_ids`: each row block 2 to 95 stands in exactly one slot; the other slots hold 96. `membership`: entries are row blocks 2 to 95, or 96 for none. `tile_pairs`: a slot's first entry is below 12, its second from 12 to 23, or both are 24 for an empty slot; over all devices every unordered pair of row blocks 2 to 96 - 1 (a block with itself too) is listed exactly once; some device fills all 20 slots.
All inputs are finite; a program needn't handle non-finite values.
Results may differ from a plain program's by a relative error of at most 0.00005.
Values sent between devices are 32-bit elements; how exact they have to be, the bound alone decides.
No kernel may reach another device: no remote copies, remote signals or barrier semaphores. Data moves between devices by JAX's collectives and lax.ppermute only.
A program may use at most 128 MiB of HBM per device.

v0:
```python
import jax
import jax.numpy as jnp
from jax import lax
from jax.sharding import PartitionSpec as P

NB = 96


def pivot_factor(matrix):
    lower_factor = jnp.linalg.cholesky(matrix)
    pivots = jnp.diagonal(lower_factor)
    identity = jnp.eye(matrix.shape[0], dtype=matrix.dtype)
    inverse = jax.scipy.linalg.solve_triangular(lower_factor, identity, lower=True)
    return (inverse.T / pivots[None, :], pivots * pivots)


def panel_factors(panel_rows, pivot_blocks, coupling, usable):
    panel_width = pivot_blocks.shape[1]
    solve_one, diag_one = pivot_factor(pivot_blocks[0])
    coupled = jnp.dot(coupling, solve_one, precision=lax.Precision.HIGHEST)
    schur = pivot_blocks[1] - jnp.dot(
        coupled * diag_one[None, :], coupled.T, precision=lax.Precision.HIGHEST
    )
    solve_two, diag_two = pivot_factor(schur)
    first = jnp.einsum(
        "rik,kj->rij", panel_rows[:, :, :panel_width], solve_one, precision=lax.Precision.HIGHEST
    )
    second_raw = panel_rows[:, :, panel_width:] - jnp.einsum(
        "rik,jk->rij", first * diag_one[None, None, :], coupled, precision=lax.Precision.HIGHEST
    )
    second = jnp.einsum("rik,kj->rij", second_raw, solve_two, precision=lax.Precision.HIGHEST)
    joined = jnp.concatenate([first, second], axis=2)
    factors = jnp.where(usable[:, None, None], joined, jnp.zeros_like(joined))
    return (factors, diag_one, diag_two)


def pair_products(group_rows, scales, tile_pairs):
    padding = jnp.zeros((1,) + group_rows.shape[1:], group_rows.dtype)
    extended = jnp.concatenate([group_rows, padding], axis=0)
    left_rows = extended[tile_pairs[:, 0]] * scales[None, None, :]
    right_rows = extended[tile_pairs[:, 1]]
    return jnp.einsum("sik,sjk->sij", left_rows, right_rows, precision=lax.Precision.HIGHEST)


def per_device(trailing_tiles, panel_rows, pivot_blocks, coupling, row_ids, membership, tile_pairs):
    owned_slots = panel_rows.shape[0]
    panel_width = pivot_blocks.shape[1]
    tile_index = lax.axis_index("tiles")
    own_ids = lax.dynamic_slice_in_dim(row_ids, tile_index * owned_slots, owned_slots)
    factors, diag_one, diag_two = panel_factors(panel_rows, pivot_blocks, coupling, own_ids < NB)
    quarter = panel_width // lax.axis_size("rep")
    my_rows = lax.dynamic_slice_in_dim(factors, lax.axis_index("rep") * quarter, quarter, 1)
    wanted = lax.dynamic_index_in_dim(membership, tile_index, 0, keepdims=False)
    picker = (wanted[:, None] == row_ids[None, :]).astype(jnp.float32)
    selected = jnp.einsum(
        "gn,nij->gij",
        picker,
        lax.all_gather(my_rows, "tiles", axis=0, tiled=True),
        precision=lax.Precision.HIGHEST,
    )
    group_rows = lax.all_gather(selected, "rep", axis=1, tiled=True)
    scales = jnp.concatenate([diag_one, diag_two])
    updated = trailing_tiles - pair_products(group_rows, scales, tile_pairs)
    return (updated, factors, jnp.stack([diag_one, diag_two]))


def solution(mesh):
    return jax.shard_map(
        per_device,
        mesh=mesh,
        in_specs=(
            P(("tiles", "rep"), None, None),
            P("tiles", None, None),
            P(),
            P(),
            P(),
            P(),
            P(("tiles", "rep"), None),
        ),
        out_specs=(P(("tiles", "rep"), None, None), P("tiles", None, None), P()),
        check_vma=False,
    )
```

profile of v0, /device:TPU:1, one launch (start us, length us, event | category | flops | bytes accessed | tf_op | source)
XLA Modules:
  0.0 469.8 jit_solution(16418581073908269618)
XLA Ops:
  9.6 11.7 %cholesky.130 = f32[128,128]{1,0:T(8,128)S(1)} custom-call(f32[128,128]{1,0:T(8,128)S(1)} %cholesky.194), custom_call_target="Cholesky" | custom-call | tf_op jit(solution)/shard_map/jit(cholesky)/cholesky | solution.py:10
  21.4 9.8 %custom-call.17 = f32[1,128,128]{1,2,0:T(8,128)S(1)} custom-call(f32[1,128,128]{2,1,0:T(8,128)S(1)} %get-tuple-element.63), custom_call_target="InvertDiagBlocksLowerTriangular" | custom-call | tf_op jit(solution)/shard_map/jit(cholesky)/cholesky | solution.py:10
  31.7 11.7 %cholesky.147 = f32[128,128]{1,0:T(8,128)S(1)} custom-call(f32[128,128]{1,0:T(8,128)S(1)} %convolution_subtract_fusion.5), custom_call_target="Cholesky" | custom-call | tf_op jit(solution)/shard_map/jit(cholesky)/cholesky | solution.py:10
  45.5 4.2 while.4
  46.3 1.4 bitcast_dynamic-update-slice_fusion.4
  48.3 1.4 bitcast_dynamic-update-slice_fusion.4
  49.7 19.7 %custom-call.18 = f32[2,128,128]{1,2,0:T(8,128)S(1)} custom-call(f32[2,128,128]{2,1,0:T(8,128)S(1)} %get-tuple-element.19), custom_call_target="InvertDiagBlocksLowerTriangular" | custom-call | tf_op jit(solution)/shard_map/jit(_solve_triangular)/triangular_solve | solution.py:13
  70.3 2.3 gather_fusion
  74.1 11.7 %cholesky.164 = f32[128,128]{1,0:T(8,128)S(1)} custom-call(f32[128,128]{1,0:T(8,128)S(1)} %cholesky.197), custom_call_target="Cholesky" | custom-call | tf_op jit(solution)/shard_map/jit(cholesky)/cholesky | solution.py:10
  85.9 9.8 %custom-call.19 = f32[1,128,128]{1,2,0:T(8,128)S(1)} custom-call(f32[1,128,128]{2,1,0:T(8,128)S(1)} %get-tuple-element.59), custom_call_target="InvertDiagBlocksLowerTriangular" | custom-call | tf_op jit(solution)/shard_map/jit(cholesky)/cholesky | solution.py:10
  96.2 11.7 %cholesky.181 = f32[128,128]{1,0:T(8,128)S(1)} custom-call(f32[128,128]{1,0:T(8,128)S(1)} %convolution_subtract_fusion.4), custom_call_target="Cholesky" | custom-call | tf_op jit(solution)/shard_map/jit(cholesky)/cholesky | solution.py:10
  110.6 4.0 while.5
  111.2 1.4 bitcast_dynamic-update-slice_fusion.5
  113.2 1.4 bitcast_dynamic-update-slice_fusion.5
  114.6 20.1 %custom-call.20 = f32[2,128,128]{1,2,0:T(8,128)S(1)} custom-call(f32[2,128,128]{2,1,0:T(8,128)S(1)} %get-tuple-element.20), custom_call_target="InvertDiagBlocksLowerTriangular" | custom-call | tf_op jit(solution)/shard_map/jit(_solve_triangular)/triangular_solve | solution.py:13
  135.6 2.3 gather_fusion.1
  141.9 103.4 %all-gather.3.cloned.1.call-done = f32[128,64,512]{2,1,0:T(8,128)} async-done(((f32[2,64,512]{2,1,0:T(8,128)}), f32[128,64,512]{2,1,0:T(8,128)}) %all-gather.3.cloned.1.call-update) | async-done | bytes 16777232 | tf_op jit(solution)/shard_map/all_gather | solution.py:58
  245.3 21.4 %fusion = f32[24,64,512]{2,0,1:T(8,128)} fusion(f32[128,64,512]{2,1,0:T(8,128)} %all-gather.3.cloned.1.call-done, s32[128]{0:T(128)S(1)} %copy-done.5, s32[24]{0:T(128)S(1)} %dynamic-slice_reduce_fusion), kind=kOutput, calls=%fused_computation.8 | convolution fusion | flops 1207962624 | bytes 19923552 | tf_op jit(solution)/shard_map/gn,nij->gij/dot_general | solution.py:55
  268.7 115.7 %all-gather.5.cloned.1.call-done = f32[24,256,512]{2,0,1:T(8,128)} async-done(((f32[24,64,512]{2,0,1:T(8,128)}), f32[24,256,512]{2,0,1:T(8,128)}) %all-gather.5.cloned.1.call-update) | async-done | bytes 12582928 | tf_op jit(solution)/shard_map/all_gather | solution.py:61
  384.4 16.4 %copy.36 = f32[24,256,512]{2,1,0:T(8,128)} copy(f32[24,256,512]{2,0,1:T(8,128)} %all-gather.5.cloned.1.call-done) | data formatting | bytes 25165824 | tf_op jit(solution)/shard_map/all_gather | solution.py:61
  400.8 11.6 %concatenate.18 = f32[25,256,512]{2,1,0:T(8,128)} pad(f32[24,256,512]{2,1,0:T(8,128)} %copy.36, f32[]{:T(128)} %constant.92.clone.1), padding=0_1x0_0x0_0 | pad | bytes 25690116 | tf_op jit(solution)/shard_map/concatenate | solution.py:39
  412.4 11.2 %gather_fusion.2 = f32[20,256,512]{2,1,0:T(8,128)} fusion(f32[25,256,512]{2,1,0:T(8,128)} %concatenate.18, s32[1024]{0:T(1024)S(1)} %get-tuple-element.73), kind=kCustom, calls=%fused_computation.2 | custom fusion | bytes 20971600 | tf_op jit(solution)/shard_map/gather | solution.py:40
  423.5 11.5 %gather_fusion.3 = f32[20,256,512]{2,1,0:T(8,128)} fusion(f32[25,256,512]{2,1,0:T(8,128)} %concatenate.18, s32[1024]{0:T(1024)S(1)} %get-tuple-element.72), kind=kCustom, calls=%fused_computation.3 | custom fusion | bytes 20971600 | tf_op jit(solution)/shard_map/gather | solution.py:41
  435.1 27.4 %fusion.5 = f32[20,256,256]{2,1,0:T(8,128)} fusion(f32[20,256,256]{2,1,0:T(8,128)} %param.10, f32[20,256,512]{2,1,0:T(8,128)} %gather_fusion.3, f32[20,256,512]{2,1,0:T(8,128)} %gather_fusion.2, f32[512]{0:T(512)S(1)} %pad_maximum_fusion), kind=kOutput, calls=%fused_computation.13 | convolution fusion | flops 8056995840 | bytes 31459328 | tf_op jit(solution)/shard_map/sik,sjk->sij/dot_general | solution.py:42
  (76 shorter events, 17.0 us)
Async XLA Ops:
  7.2 65.7 %copy-start = (f32[256,256]{1,0:T(8,128)S(1)}, f32[256,256]{1,0:T(8,128)}, u32[]{:S(2)}) copy-start(f32[256,256]{1,0:T(8,128)} %param.13) | copy-start | bytes 786436
  7.2 130.7 %copy-start.2 = (f32[2,256,512]{2,1,0:T(8,128)S(1)}, f32[2,256,512]{2,1,0:T(8,128)}, u32[]{:S(2)}) copy-start(f32[2,256,512]{2,1,0:T(8,128)} %param.11) | copy-start | bytes 3145732
  7.2 132.5 %copy-start.5 = (s32[128]{0:T(128)S(1)}, s32[128]{0:T(128)}, u32[]{:S(2)}) copy-start(s32[128]{0:T(128)} %param.14) | copy-start | bytes 1540
  7.2 238.1 %all-gather.3.cloned.1.call-start = ((), (), s32[]{:S(2)}) async-start(), calls=%async_computation | async-start | bytes 17039360 | tf_op jit(solution)/shard_map/all_gather | solution.py:58
  45.5 96.2 %copy-start.3 = (s32[64,24]{0,1:T(8,128)S(1)}, s32[64,24]{0,1:T(8,128)}, u32[]{:S(2)}) copy-start(s32[64,24]{0,1:T(8,128)} %param.15) | copy-start | bytes 18436
  141.7 242.7 %all-gather.5.cloned.1.call-start = ((), (), s32[]{:S(2)}) async-start(), calls=%async_computation.1 | async-start | bytes 15728640 | tf_op jit(solution)/shard_map/all_gather | solution.py:61
  141.9 126.7 %copy-start.4 = (s32[20,2]{0,1:T(2,128)S(1)}, s32[20,2]{0,1:T(2,128)}, u32[]{:S(2)}) copy-start(s32[20,2]{0,1:T(2,128)} %param.16) | copy-start | bytes 484
  423.5 38.9 %copy-start.1 = (f32[256,256]{1,0:T(8,128)S(1)}, f32[256,256]{1,0:T(8,128)}, u32[]{:S(2)}) copy-start(f32[256,256]{1,0:T(8,128)} %param.13) | copy-start | bytes 786436
Sparse Core Ops, SparseCore 0:
  141.8 103.4 all-gather.2
  266.9 117.4 all-gather.4
where the time goes:
time: 478 us; the launch traced here: 470 us
  waiting for transfers between devices  219 us (46%)
  other arithmetic  110 us (23%)
  local copies, waits for them, and re-layouts  67.5 us (14%)
  matrix products  55 us (12%)
  between operations  17.5 us (4%)
    all_gather x1, waiting for transfers between devices, per_device(): group_rows = lax.all_gather(selected, 'rep', axis=1, tiled=True)  116 us
    all_gather x1, waiting for transfers between devices, per_device(): lax.all_gather(my_rows, 'tiles', axis=0, tiled=True)  103 us
    another operation x13, other arithmetic, pivot_factor(): lower_factor = jnp.linalg.cholesky(matrix)  68.5 us
    another operation x5, other arithmetic, pivot_factor(): jax.scipy.linalg.solve_triangular(lower_factor, identity, lower=True)  39.8 us
    dot_general x1, matrix products, pair_products(): jnp.einsum('sik,sjk->sij', left_rows, right_rows, precision=lax.Precision...  27.4 us
    dot_general x1, matrix products, per_device(): jnp.einsum('gn,nij->gij', picker, lax.all_gather(my_rows, 'tiles', axis=0...  21.4 us
    all_gather x1, local copies, waits for them, and re-layouts, per_device(): group_rows = lax.all_gather(selected, 'rep', axis=1, tiled=True)  16.4 us
    concatenate x1, local copies, waits for them, and re-layouts, pair_products(): extended = jnp.concatenate([group_rows, padding], axis=0)  11.6 us
  transfers between devices with their start and end apart: 2, of which 2 were waited for; matrix products, arithmetic and copies ran while one was open for 0% of the time, Pallas kernels for 0%

commit v1 on v0

--- a/solution.py
+++ b/solution.py
@@ -55,7 +55,9 @@
     selected = jnp.einsum(
         "gn,nij->gij",
         picker,
-        lax.all_gather(my_rows, "tiles", axis=0, tiled=True),
+        jnp.concatenate(
+            lax.all_to_all(jnp.stack([my_rows] * lax.axis_size("tiles")), "tiles", 0, 0), axis=0
+        ),
         precision=lax.Precision.HIGHEST,
     )
     group_rows = lax.all_gather(selected, "rep", axis=1, tiled=True)

time: 478 us -> 792 us (1.66)
  waiting for transfers between devices: 219 us -> 481 us
  local copies, waits for them, and re-layouts: 67.5 us -> 109 us
  starting transfers between devices: 0.08 us -> 13.5 us
  matrix products: 55 us -> 43.9 us
  other arithmetic: 110 us -> 118 us
    all_to_all x0 -> x1, waiting for transfers between devices: none -> 365 us  [per_device(): lax.all_to_all(jnp.stack([my_rows] * lax.axis_size('tiles')), 'tiles', 0, 0)]
    all_gather x1 -> x0, waiting for transfers between devices: 103 us -> none  [per_device(): lax.all_gather(my_rows, 'tiles', axis=0, tiled=True)]
    reshape x0 -> x1, local copies, waits for them, and re-layouts: none -> 20.5 us  [per_device(): jnp.concatenate(lax.all_to_all(jnp.stack([my_rows] * lax.axis_size('tiles...]
    all_to_all x0 -> x1, starting transfers between devices: none -> 13.5 us  [per_device(): lax.all_to_all(jnp.stack([my_rows] * lax.axis_size('tiles')), 'tiles', 0, 0)]
    all_to_all x0 -> x1, local copies, waits for them, and re-layouts: none -> 12 us  [per_device(): lax.all_to_all(jnp.stack([my_rows] * lax.axis_size('tiles')), 'tiles', 0, 0)]
    dot_general x1, matrix products: 21.4 us -> 10.3 us  [per_device(): jnp.einsum('gn,nij->gij', picker, jnp.concatenate(lax.all_to_all(jnp.stac...]
    another operation x0 -> x1, local copies, waits for them, and re-layouts: none -> 9.34 us  [per_device(): jnp.stack([my_rows] * lax.axis_size('tiles'))]
    another operation x5, other arithmetic: 39.8 us -> 47.9 us  [pivot_factor(): jax.scipy.linalg.solve_triangular(lower_factor, identity, lower=True)]
where the time goes in v1:
time: 792 us; the launch traced here: 783 us
  waiting for transfers between devices  481 us (61%)
  other arithmetic  118 us (15%)
  local copies, waits for them, and re-layouts  109 us (14%)
  matrix products  43.9 us (6%)
  between operations  17.5 us (2%)
  starting transfers between devices  13.5 us (2%)
    all_to_all x1, waiting for transfers between devices, per_device(): lax.all_to_all(jnp.stack([my_rows] * lax.axis_size('tiles')), 'tiles', 0, 0)  365 us
    all_gather x1, waiting for transfers between devices, per_device(): group_rows = lax.all_gather(selected, 'rep', axis=1, tiled=True)  116 us
    another operation x13, other arithmetic, pivot_factor(): lower_factor = jnp.linalg.cholesky(matrix)  68.5 us
    another operation x5, other arithmetic, pivot_factor(): jax.scipy.linalg.solve_triangular(lower_factor, identity, lower=True)  47.9 us
    dot_general x1, matrix products, pair_products(): jnp.einsum('sik,sjk->sij', left_rows, right_rows, precision=lax.Precision...  27.4 us
    reshape x1, local copies, waits for them, and re-layouts, per_device(): jnp.concatenate(lax.all_to_all(jnp.stack([my_rows] * lax.axis_size('tiles...  20.5 us
    all_gather x1, local copies, waits for them, and re-layouts, per_device(): group_rows = lax.all_gather(selected, 'rep', axis=1, tiled=True)  16.4 us
  transfers between devices with their start and end apart: 2, of which 2 were waited for; matrix products, arithmetic and copies ran while one was open for 0% of the time, Pallas kernels for 0%

profile of v1, /device:TPU:1, one launch (start us, length us, event | category | flops | bytes accessed | tf_op | source)
XLA Modules:
  0.0 783.1 jit_solution(13617573584774594209)
XLA Ops:
  9.6 11.7 %cholesky.130 = f32[128,128]{1,0:T(8,128)S(1)} custom-call(f32[128,128]{1,0:T(8,128)S(1)} %cholesky.194), custom_call_target="Cholesky" | custom-call | tf_op jit(solution)/shard_map/jit(cholesky)/cholesky | solution.py:10
  21.3 9.8 %custom-call.17 = f32[1,128,128]{1,2,0:T(8,128)S(1)} custom-call(f32[1,128,128]{2,1,0:T(8,128)S(1)} %get-tuple-element.63), custom_call_target="InvertDiagBlocksLowerTriangular" | custom-call | tf_op jit(solution)/shard_map/jit(cholesky)/cholesky | solution.py:10
  31.6 11.7 %cholesky.147 = f32[128,128]{1,0:T(8,128)S(1)} custom-call(f32[128,128]{1,0:T(8,128)S(1)} %convolution_subtract_fusion.5), custom_call_target="Cholesky" | custom-call | tf_op jit(solution)/shard_map/jit(cholesky)/cholesky | solution.py:10
  45.5 4.3 while.4
  49.7 19.7 %custom-call.18 = f32[2,128,128]{1,2,0:T(8,128)S(1)} custom-call(f32[2,128,128]{2,1,0:T(8,128)S(1)} %get-tuple-element.19), custom_call_target="InvertDiagBlocksLowerTriangular" | custom-call | tf_op jit(solution)/shard_map/jit(_solve_triangular)/triangular_solve | solution.py:13
  70.3 2.3 gather_fusion
  74.1 11.7 %cholesky.164 = f32[128,128]{1,0:T(8,128)S(1)} custom-call(f32[128,128]{1,0:T(8,128)S(1)} %cholesky.197), custom_call_target="Cholesky" | custom-call | tf_op jit(solution)/shard_map/jit(cholesky)/cholesky | solution.py:10
  85.9 9.8 %custom-call.19 = f32[1,128,128]{1,2,0:T(8,128)S(1)} custom-call(f32[1,128,128]{2,1,0:T(8,128)S(1)} %get-tuple-element.59), custom_call_target="InvertDiagBlocksLowerTriangular" | custom-call | tf_op jit(solution)/shard_map/jit(cholesky)/cholesky | solution.py:10
  96.2 11.7 %cholesky.181 = f32[128,128]{1,0:T(8,128)S(1)} custom-call(f32[128,128]{1,0:T(8,128)S(1)} %convolution_subtract_fusion.4), custom_call_target="Cholesky" | custom-call | tf_op jit(solution)/shard_map/jit(cholesky)/cholesky | solution.py:10
  110.6 4.0 while.5
  114.6 28.1 %custom-call.20 = f32[2,128,128]{1,2,0:T(8,128)S(1)} custom-call(f32[2,128,128]{2,1,0:T(8,128)S(1)} %get-tuple-element.20), custom_call_target="InvertDiagBlocksLowerTriangular" | custom-call | tf_op jit(solution)/shard_map/jit(_solve_triangular)/triangular_solve | solution.py:13
  143.6 2.3 gather_fusion.1
  149.0 9.3 %stack.4 = f32[64,2,64,512]{3,1,2,0:T(2,128)} broadcast(f32[2,64,512]{2,0,1:T(2,128)S(1)} %copy.34), dimensions={1,2,3} | broadcast | bytes 17039360 | tf_op jit(solution)/shard_map/stack | solution.py:59
  158.3 13.5 %all-to-all-start = ((f32[64,2,64,512]{3,1,2,0:T(2,128)}), f32[64,2,64,512]{3,1,2,0:T(2,128)}, u32[]{:S(2)}, u32[]{:S(2)}) async-start(f32[64,2,64,512]{3,1,2,0:T(2,128)} %stack.4), calls=%async_computation | async-start | bytes 33554432 | tf_op jit(solution)/shard_map/all_to_all | solution.py:59
  172.1 365.3 %all-to-all-done = f32[64,2,64,512]{3,1,2,0:T(2,128)} async-done(((f32[64,2,64,512]{3,1,2,0:T(2,128)}), f32[64,2,64,512]{3,1,2,0:T(2,128)}, u32[]{:S(2)}, u32[]{:S(2)}) %all-to-all-start) | async-done | bytes 16777248 | tf_op jit(solution)/shard_map/all_to_all | solution.py:59
  537.3 12.0 %copy.35 = f32[64,2,64,512]{3,1,0,2:T(2,128)} copy(f32[64,2,64,512]{3,1,2,0:T(2,128)} %all-to-all-done) | data formatting | bytes 33554432 | tf_op jit(solution)/shard_map/all_to_all | solution.py:59
  549.3 20.5 %reshape.52 = f32[128,64,512]{2,0,1:T(8,128)} reshape(f32[64,2,64,512]{3,1,0,2:T(2,128)} %copy.35) | data formatting | bytes 33554432 | tf_op jit(solution)/shard_map/reshape | solution.py:58
  569.9 10.3 %fusion.39 = f32[24,64,512]{2,0,1:T(8,128)} fusion(f32[128,64,512]{2,0,1:T(8,128)} %reshape.52, s32[128]{0:T(128)S(1)} %copy-done.5, s32[24]{0:T(128)S(1)} %dynamic-slice_reduce_fusion), kind=kOutput, calls=%fused_computation.72 | convolution fusion | flops 1207962624 | bytes 19923552 | tf_op jit(solution)/shard_map/gn,nij->gij/dot_general | solution.py:55
  582.2 115.6 %all-gather.2.cloned.1.call-done = f32[24,256,512]{2,0,1:T(8,128)} async-done(((f32[24,64,512]{2,0,1:T(8,128)}), f32[24,256,512]{2,0,1:T(8,128)}) %all-gather.2.cloned.1.call-update) | async-done | bytes 12582928 | tf_op jit(solution)/shard_map/all_gather | solution.py:63
  697.8 16.4 %copy.36 = f32[24,256,512]{2,1,0:T(8,128)} copy(f32[24,256,512]{2,0,1:T(8,128)} %all-gather.2.cloned.1.call-done) | data formatting | bytes 25165824 | tf_op jit(solution)/shard_map/all_gather | solution.py:63
  714.2 11.6 %concatenate.18 = f32[25,256,512]{2,1,0:T(8,128)} pad(f32[24,256,512]{2,1,0:T(8,128)} %copy.36, f32[]{:T(128)} %constant.92.clone.1), padding=0_1x0_0x0_0 | pad | bytes 25690116 | tf_op jit(solution)/shard_map/concatenate | solution.py:39
  725.8 11.2 %gather_fusion.2 = f32[20,256,512]{2,1,0:T(8,128)} fusion(f32[25,256,512]{2,1,0:T(8,128)} %concatenate.18, s32[1024]{0:T(1024)S(1)} %get-tuple-element.73), kind=kCustom, calls=%fused_computation.2 | custom fusion | bytes 20971600 | tf_op jit(solution)/shard_map/gather | solution.py:40
  736.9 11.5 %gather_fusion.3 = f32[20,256,512]{2,1,0:T(8,128)} fusion(f32[25,256,512]{2,1,0:T(8,128)} %concatenate.18, s32[1024]{0:T(1024)S(1)} %get-tuple-element.72), kind=kCustom, calls=%fused_computation.3 | custom fusion | bytes 20971600 | tf_op jit(solution)/shard_map/gather | solution.py:41
  748.4 27.4 %fusion.3 = f32[20,256,256]{2,1,0:T(8,128)} fusion(f32[20,256,256]{2,1,0:T(8,128)} %param.10, f32[20,256,512]{2,1,0:T(8,128)} %gather_fusion.3, f32[20,256,512]{2,1,0:T(8,128)} %gather_fusion.2, f32[512]{0:T(512)S(1)} %pad_maximum_fusion), kind=kOutput, calls=%fused_computation.11 | convolution fusion | flops 8056995840 | bytes 31459328 | tf_op jit(solution)/shard_map/sik,sjk->sij/dot_general | solution.py:42
  (78 shorter events, 21.8 us)
Async XLA Ops:
  7.2 65.7 %copy-start = (f32[256,256]{1,0:T(8,128)S(1)}, f32[256,256]{1,0:T(8,128)}, u32[]{:S(2)}) copy-start(f32[256,256]{1,0:T(8,128)} %param.13) | copy-start | bytes 786436
  7.2 138.8 %copy-start.2 = (f32[2,256,512]{2,1,0:T(8,128)S(1)}, f32[2,256,512]{2,1,0:T(8,128)}, u32[]{:S(2)}) copy-start(f32[2,256,512]{2,1,0:T(8,128)} %param.11) | copy-start | bytes 3145732
  7.2 140.5 %copy-start.5 = (s32[128]{0:T(128)S(1)}, s32[128]{0:T(128)}, u32[]{:S(2)}) copy-start(s32[128]{0:T(128)} %param.14) | copy-start | bytes 1540
  158.3 13.5 %copy-start.3 = (s32[64,24]{0,1:T(8,128)S(1)}, s32[64,24]{0,1:T(8,128)}, u32[]{:S(2)}) copy-start(s32[64,24]{0,1:T(8,128)} %param.15) | copy-start | bytes 18436
  158.3 379.0 %all-to-all-start = ((f32[64,2,64,512]{3,1,2,0:T(2,128)}), f32[64,2,64,512]{3,1,2,0:T(2,128)}, u32[]{:S(2)}, u32[]{:S(2)}) async-start(f32[64,2,64,512]{3,1,2,0:T(2,128)} %stack.4), calls=%async_computation | async-start | bytes 33554432 | tf_op jit(solution)/shard_map/all_to_all | solution.py:59
  171.8 526.0 %all-gather.2.cloned.1.call-start = ((), (), s32[]{:S(2)}) async-start(), calls=%async_computation.1 | async-start | bytes 15728640 | tf_op jit(solution)/shard_map/all_gather | solution.py:63
  569.9 12.3 %copy-start.4 = (s32[20,2]{0,1:T(2,128)S(1)}, s32[20,2]{0,1:T(2,128)}, u32[]{:S(2)}) copy-start(s32[20,2]{0,1:T(2,128)} %param.16) | copy-start | bytes 484
  736.9 38.9 %copy-start.1 = (f32[256,256]{1,0:T(8,128)S(1)}, f32[256,256]{1,0:T(8,128)}, u32[]{:S(2)}) copy-start(f32[256,256]{1,0:T(8,128)} %param.13) | copy-start | bytes 786436
Sparse Core Ops, SparseCore 0:
  580.4 117.3 all-gather.1
